TPU v7x, 128 devices: a whole 4x4x4 slice. The times are simulated.
128 devices in a mesh: hemi: 2 (over core), blk: 64 (over x, z, y).
Axes of the slice: x: 4, y: 4, z: 4, core: 2. Of those that a mesh axis runs over, the one named last changes fastest.
Arguments:
- data: float32 [2, 256, 256, 2, 256], P('hemi', 'blk'), may hold values from -6 to 6
- signal: float32 [2, 256, 256, 2, 256], P('hemi', 'blk'), may hold values from -6 to 6
- noise: float32 [2, 256], P('hemi', 'blk'), may hold values from 0.5 to 48
- cycle_weight: float32 [256], replicated, may hold values from 2 to 8
- cl: float32 [16384], replicated, may hold values from 0.05 to 20
- legendre: bfloat16 [256, 2, 256, 8192], P('blk', 'hemi'), may hold values from -0.0625 to 0.0625
- m_table: int32 [256], P('blk'), may hold values from 0 to 16383, as said below
Outputs:
- new_signal: float32 [2, 256, 256, 2, 256], P('hemi', 'blk')
Inputs may be any that keep to these rules, and one draw needn't show every extreme that they name: `m_table`: the 256 entries are distinct; which slot holds which order is drawn.
All inputs are finite; a program needn't handle non-finite values.
Results may differ from a plain program's by a relative error of at most 0.003.
Values sent between devices are 32-bit elements; how exact they have to be, the bound alone decides.
No kernel may reach another device: no remote copies, remote signals or barrier semaphores. Data moves between devices by JAX's collectives and lax.ppermute only.
A program may use at most 128 MiB of HBM per device.

v0:
```python
import jax
import jax.numpy as jnp
from jax import lax
from jax.experimental import pallas as pl
from jax.experimental.pallas import tpu as pltpu
from jax.sharding import PartitionSpec as P

ALL = ("blk", "hemi")
BLK = 64
DEV = 128
SLOTS = 4
CYCLES = 256
COLS = 8192
UNIT = 512
UNIT_BITS = 9
SIZES = (4096, 2048, 1024, 512)
LANES = 128
SWAP = [(0, 1), (1, 0)]


def to_tiles(array):
    array = array.reshape(4, 256, 2, 2, LANES).transpose(0, 1, 3, 2, 4)
    return array.reshape(2, 2, BLK, 2, 8, LANES)


def from_tiles(array):
    return array.reshape(4, 256, 2, 2, LANES).transpose(0, 1, 3, 2, 4).reshape(1, 4, 256, 2, 256)


BIG = 3e38
VMEM_ALL = 67043328


STAGES = 4


def messenger_kernel(all_noise_ref, weight_hbm, data, signal, data2, signal2, out, ins, sums, weights, in_sem, out_sem, weight_sem):
    hemi = lax.axis_index("hemi")
    blk = lax.axis_index("blk")
    step = BLK // STAGES
    sources = (data, signal, data2, signal2)

    def fetch(n, i):
        at = pl.ds(i * step, step)
        return pltpu.make_async_copy(sources[n].at[hemi, :, at], ins.at[n, :, at], in_sem.at[n, i])

    def store(i):
        at = pl.ds(i * step, step)
        return pltpu.make_async_copy(sums.at[at], out.at[at], out_sem.at[i])

    weight_copy = pltpu.make_async_copy(weight_hbm, weights, weight_sem)
    weight_copy.start()
    for i in range(STAGES):
        for n in range(4):
            fetch(n, i).start()
    sign = (1 - 2 * hemi).astype(jnp.float32)
    tau = jnp.min(all_noise_ref[...])
    lane = lax.broadcasted_iota(jnp.int32, (1, LANES), 1)
    own_row = all_noise_ref[pl.ds(2 * blk + hemi, 1), :]
    other_row = all_noise_ref[pl.ds(2 * blk + 1 - hemi, 1), :]

    def pick(row, at):
        return jnp.sum(jnp.where(lane == at, row, 0.0), axis=1, keepdims=True)

    coefs = []
    first = 4 * blk + 2 * hemi
    weight_copy.wait()
    weight_row = weights[pl.ds(first >> 7, 1), :]
    for r in range(2):
        weight = pick(weight_row, (first & 127) + r)
        for n in (pick(own_row, 2 * hemi + r), pick(other_row, 2 * hemi + r)):
            scale = weight / n
            coefs.append((jnp.broadcast_to(scale * tau, (8, LANES)), jnp.broadcast_to(scale * (n - tau), (8, LANES))))
    small = 4
    for i in range(STAGES):
        for n in range(4):
            fetch(n, i).wait()

        @pl.loop(0, step // small)
        def _(j, i=i):
            at = pl.ds(i * step + j * small, small)
            for r in range(2):
                (a, b), (a2, b2) = coefs[2 * r:2 * r + 2]
                for kk in range(2):
                    own = a * ins[0, r, at, kk] + b * ins[1, r, at, kk]
                    other = a2 * ins[2, r, at, kk] + b2 * ins[3, r, at, kk]
                    sums[at, 0, r, kk] = own + other
                    sums[at, 1, r, kk] = sign * (own - other)

        store(i).start()
    for i in range(STAGES):
        store(i).wait()


def messenger(all_noise, weight, data, signal, data2, signal2):
    hbm = pl.BlockSpec(memory_space=pltpu.HBM)
    return pl.pallas_call(
        messenger_kernel,
        in_specs=[pl.BlockSpec(memory_space=pltpu.VMEM)] + [hbm] * 5,
        out_specs=hbm,
        out_shape=jax.ShapeDtypeStruct((BLK, 2, 2, 2, 8, LANES), jnp.float32),
        scratch_shapes=[
            pltpu.VMEM((4, 2, BLK, 2, 8, LANES), jnp.float32),
            pltpu.VMEM((BLK, 2, 2, 2, 8, LANES), jnp.float32),
            pltpu.VMEM((2, LANES), jnp.float32),
            pltpu.SemaphoreType.DMA((4, STAGES)),
            pltpu.SemaphoreType.DMA((STAGES,)),
            pltpu.SemaphoreType.DMA,
        ],
        compiler_params=pltpu.CompilerParams(vmem_limit_bytes=VMEM_ALL),
        cost_estimate=pl.CostEstimate(flops=4 << 20, bytes_accessed=6 << 20, transcendentals=0),
        name="messenger",
    )(all_noise, weight, data, signal, data2, signal2)


def prepare_kernel(m_ref, cl_ref, out_ref, mixed, picked):
    hemi = lax.axis_index("hemi")
    src = lax.broadcasted_iota(jnp.int32, (LANES, LANES), 0)
    dst = lax.broadcasted_iota(jnp.int32, (LANES, LANES), 1)
    pick = jnp.where(src == 2 * (dst & 63) + (dst >> 6), 1.0, 0.0).astype(jnp.float32)
    mixed[...] = jnp.dot(cl_ref[...], pick, precision=lax.Precision.HIGHEST, preferred_element_type=jnp.float32)
    low = mixed[pl.ds(0, 64, stride=2), :]
    high = mixed[pl.ds(1, 64, stride=2), :]
    lane = lax.broadcasted_iota(jnp.int32, (64, LANES), 1)
    picked[...] = jnp.zeros_like(picked)
    picked[0, 0:64, :] = jnp.where(lane < 64, low, pltpu.roll(high, 64, 1))
    picked[1, 0:64, :] = jnp.where(lane < 64, pltpu.roll(low, 64, 1), high)
    for slot in range(SLOTS):
        start = (m_ref[slot] + hemi) >> 1
        parity = (m_ref[slot] + hemi) & 1
        row, turn = start >> 7, start & 127
        back = (LANES - turn) & 127
        here = pltpu.roll(picked[parity, pl.ds(row, 64), :], back, 1)
        after = pltpu.roll(picked[parity, pl.ds(row + 1, 64), :], back, 1)
        out_ref[slot] = jnp.where(lane < LANES - turn, here, after)


def prepare(m_table, cl):
    smem = pl.BlockSpec(memory_space=pltpu.SMEM)
    vmem = pl.BlockSpec(memory_space=pltpu.VMEM)
    return pl.pallas_call(
        prepare_kernel,
        in_specs=[smem, vmem],
        out_specs=vmem,
        out_shape=jax.ShapeDtypeStruct((SLOTS, 64, LANES), jnp.float32),
        scratch_shapes=[pltpu.VMEM((LANES, LANES), jnp.float32), pltpu.VMEM((2, 136, LANES), jnp.float32)],
        compiler_params=pltpu.CompilerParams(vmem_limit_bytes=4 << 20),
        cost_estimate=pl.CostEstimate(flops=4 << 20, bytes_accessed=1 << 18, transcendentals=0),
        name="prepare",
    )(m_table, cl)


def filter_kernel(m_ref, all_noise_ref, cl_ref, rows_ref, leg_hbm, out_ref, leg, halves, acc, gain, leg_sem):
    hemi = lax.axis_index("hemi")
    stride = 4 * SLOTS

    def units_of(slot):
        return (COLS - ((m_ref[slot] + hemi) >> 1) + UNIT - 1) >> UNIT_BITS

    def fetch(slot, j):
        cols = pl.ds(pl.multiple_of(j * UNIT, UNIT), UNIT)
        return pltpu.make_async_copy(leg_hbm.at[slot, :, cols], leg.at[slot, :, cols], leg_sem.at[slot, j])

    for slot in range(SLOTS):
        @pl.loop(0, units_of(slot))
        def _(j, slot=slot):
            fetch(slot, j).start()

    tau = jnp.min(all_noise_ref[...])

    @pl.loop(0, SLOTS)
    def _(slot):
        for q in range(4):
            part = rows_ref[pl.ds(slot * 4 + q, CYCLES, stride=stride), :]
            halves[slot, q * LANES:(q + 1) * LANES, :] = part.T.astype(jnp.bfloat16)

    def block(slot, at, size):
        @pl.loop(0, size // UNIT)
        def _(i):
            fetch(slot, at + i).wait()

        table = leg[slot, :, pl.ds(pl.multiple_of(at * UNIT, UNIT), size)]
        coeffs = jnp.dot(halves[slot], table, preferred_element_type=jnp.float32)
        row_of = [gain[pl.ds(at * (UNIT // LANES) + i, 1), :] for i in range(size // LANES)]
        filtered = (coeffs * jnp.concatenate(row_of, axis=1)).astype(jnp.bfloat16)
        acc[...] += lax.dot_general(table, filtered, (((1,), (1,)), ((), ())), preferred_element_type=jnp.float32)

    @pl.loop(0, SLOTS)
    def _(slot):
        units = units_of(slot)
        cl_cols = cl_ref[slot]
        gain[...] = cl_cols / (cl_cols + tau)
        acc[...] = jnp.zeros_like(acc)
        per = SIZES[0] // UNIT
        whole = units >> (per.bit_length() - 1)

        @pl.loop(0, whole)
        def _(j):
            block(slot, j * per, SIZES[0])

        at = whole * per
        for size in SIZES[1:]:
            per = size // UNIT

            @pl.when((units & per) != 0)
            def _(at=at, size=size):
                block(slot, at, size)

            at = at + (units & per)
        for q in range(4):
            out_ref[pl.ds(slot * 4 + q, CYCLES, stride=stride), :] = acc[:, q * LANES:(q + 1) * LANES]


def filtering(m_table, all_noise, cl_cols, rows, legendre):
    smem = pl.BlockSpec(memory_space=pltpu.SMEM)
    vmem = pl.BlockSpec(memory_space=pltpu.VMEM)
    hbm = pl.BlockSpec(memory_space=pltpu.HBM)
    return pl.pallas_call(
        filter_kernel,
        in_specs=[smem, vmem, vmem, vmem, hbm],
        out_specs=vmem,
        out_shape=jax.ShapeDtypeStruct((CYCLES * 16, LANES), jnp.float32),
        scratch_shapes=[
            pltpu.VMEM((SLOTS, CYCLES, COLS), jnp.bfloat16),
            pltpu.VMEM((SLOTS, 512, CYCLES), jnp.bfloat16),
            pltpu.VMEM((CYCLES, 512), jnp.float32),
            pltpu.VMEM((64, LANES), jnp.float32),
            pltpu.SemaphoreType.DMA((SLOTS, COLS // UNIT)),
        ],
        compiler_params=pltpu.CompilerParams(vmem_limit_bytes=44 << 20),
        cost_estimate=pl.CostEstimate(flops=16 << 30, bytes_accessed=20 << 20, transcendentals=0),
        name="filtering",
    )(m_table, all_noise, cl_cols, rows, legendre)


def combine_kernel(own, parts, out, *scratch):
    hemi = lax.axis_index("hemi")
    sign = (1 - 2 * hemi).astype(jnp.float32)
    if not own:
        sign = -sign
    target = scratch[0] if own else out
    small = 8

    @pl.loop(0, BLK // small)
    def _(i):
        at = pl.ds(i * small, small)
        for r in range(2):
            for kk in range(2):
                target[r, at, kk] = parts[at, 0, r, kk] + sign * parts[at, 1, r, kk]

    if own:
        copy = pltpu.make_async_copy(scratch[0], out.at[hemi], scratch[1])
        copy.start()
        copy.wait()


def combine(parts, own):
    half = (2, BLK, 2, 8, LANES)
    vmem = pl.BlockSpec(memory_space=pltpu.VMEM)

    def body(*refs):
        combine_kernel(own, *refs)

    return pl.pallas_call(
        body,
        in_specs=[vmem],
        out_specs=pl.BlockSpec(memory_space=pltpu.HBM) if own else vmem,
        out_shape=jax.ShapeDtypeStruct((2,) + half if own else half, jnp.float32),
        scratch_shapes=[pltpu.VMEM(half, jnp.float32), pltpu.SemaphoreType.DMA] if own else [],
        compiler_params=pltpu.CompilerParams(vmem_limit_bytes=6 << 20),
        cost_estimate=pl.CostEstimate(flops=1 << 20, bytes_accessed=3 << 20, transcendentals=0),
        name="combine_own" if own else "combine_other",
    )(parts)


def place_kernel(part_ref, whole_ref, out_ref, sem):
    copy = pltpu.make_async_copy(part_ref, out_ref.at[1 - lax.axis_index("hemi")], sem)
    copy.start()
    copy.wait()


def place(part, whole):
    hbm = pl.BlockSpec(memory_space=pltpu.HBM)
    return pl.pallas_call(
        place_kernel,
        in_specs=[pl.BlockSpec(memory_space=pltpu.VMEM), hbm],
        out_specs=hbm,
        out_shape=jax.ShapeDtypeStruct(whole.shape, jnp.float32),
        scratch_shapes=[pltpu.SemaphoreType.DMA],
        input_output_aliases={1: 0},
        compiler_params=pltpu.CompilerParams(vmem_limit_bytes=4 << 20),
        cost_estimate=pl.CostEstimate(flops=0, bytes_accessed=2 << 20, transcendentals=0),
        name="place",
    )(part, whole)


def shards(data, signal, noise, cycle_weight, cl, legendre, m_table):
    seen = jnp.broadcast_to(jnp.pad(noise, ((0, 0), (0, LANES - 4)), constant_values=BIG)[None], (DEV, 1, LANES))
    all_noise = lax.all_to_all(seen, ALL, 0, 0, tiled=True).reshape(DEV, LANES)
    data, signal = to_tiles(data), to_tiles(signal)
    data2 = lax.ppermute(data, "hemi", SWAP)
    signal2 = lax.ppermute(signal, "hemi", SWAP)
    sums = messenger(all_noise, cycle_weight.reshape(2, LANES), data, signal, data2, signal2)
    cl_cols = prepare(m_table, cl.reshape(LANES, LANES))
    modes = lax.all_to_all(sums.reshape(DEV, 32, LANES), ALL, 0, 0, tiled=True)
    done = filtering(m_table, all_noise, cl_cols, modes.reshape(CYCLES * 16, LANES), legendre.reshape(SLOTS, CYCLES, COLS))
    back = lax.all_to_all(done.reshape(DEV, 32, LANES), ALL, 0, 0, tiled=True)
    parts = back.reshape(BLK, 2, 2, 2, 8, LANES)
    sent = lax.ppermute(combine(parts, False), "hemi", SWAP)
    whole = combine(parts, True)
    return from_tiles(place(sent, whole))


def solution(mesh):
    return jax.shard_map(
        shards,
        mesh=mesh,
        in_specs=(
            P("hemi", "blk", None, None, None),
            P("hemi", "blk", None, None, None),
            P("hemi", "blk"),
            P(),
            P(),
            P("blk", "hemi", None, None),
            P("blk"),
        ),
        out_specs=P("hemi", "blk", None, None, None),
        check_vma=False,
    )
```

profile of v0, /device:TPU:1, one launch (start us, length us, event | category | flops | bytes accessed | tf_op | source)
XLA Modules:
  0.0 121.2 jit_solution(9650665130262989739)
XLA Ops:
  0.0 1.4 %collective-permute-start = (f32[2,2,64,2,8,128]{5,4,3,2,1,0:T(8,128)}, f32[2,2,64,2,8,128]{5,4,3,2,1,0:T(8,128)}, u32[]{:S(2)}, u32[]{:S(2)}) collective-permute-start(f32[2,2,64,2,8,128]{5,4,3,2,1,0:T(8,128)} %bitcast.33), channel_id=1, source_target_pairs={{0,64},{64,0},{1,65},{65,1},{2,66},{66,2},{3,67},{67,3},{4,68},{68... | collective-permute-start | bytes 6291464 | tf_op jit(solution)/shard_map/ppermute | solution.py:301
  1.4 0.0 collective-permute-start.1
  1.4 0.7 pad_bitcast_fusion
  2.1 20.3 %all_to_all.15 = f32[128,1,128]{2,1,0:T(1,128)} all-to-all(f32[128,1,128]{2,1,0:T(1,128)S(1)} %broadcast_in_dim.9), channel_id=1, replica_groups=mesh['hemi'=2,'blk'=64] {'blk','hemi'}, dimensions={0} | all-to-all | bytes 131072 | tf_op jit(solution)/shard_map/all_to_all | solution.py:299
  22.4 0.0 collective-permute-done.data2
  22.4 0.0 collective-permute-done.1.signal2
  22.4 4.4 %messenger.1 = f32[64,2,2,2,8,128]{5,4,3,2,1,0:T(8,128)} custom-call(f32[128,128]{1,0:T(8,128)} %bitcast.29, f32[2,128]{1,0:T(2,128)} %bitcast.37, f32[2,2,64,2,8,128]{5,4,3,2,1,0:T(8,128)} %bitcast.34, f32[2,2,64,2,8,128]{5,4,3,2,1,0:T(8,128)} %bitcast.36, f32[2,2,64,2,8,128]{5,4,3,2,1,0:T(8,128)} %collective-permute-done.data2, ...), custom_call_target="tpu_custom_call" | custom-call | flops 4194304 | bytes 6291456 | tf_op jit(solution)/shard_map/messenger/pallas_call | solution.py:97
  26.8 0.0 copy-start.1
  26.8 0.0 copy-start.2
  26.8 0.0 copy-start
  26.8 4.8 %all-to-all-start.1 = ((f32[128,32,128]{2,1,0:T(8,128)}), f32[128,32,128]{2,1,0:T(8,128)S(1)}, u32[]{:S(2)}, u32[]{:S(2)}) async-start(f32[128,32,128]{2,1,0:T(8,128)} %bitcast.32), calls=%async_computation.1 | async-start | bytes 4194304 | tf_op jit(solution)/shard_map/all_to_all | solution.py:305
  31.6 0.0 copy-done.1
  31.6 0.0 copy-done.2
  31.6 1.0 prepare.1.cl_ref
  32.6 29.2 %all-to-all-done.1 = f32[128,32,128]{2,1,0:T(8,128)S(1)} async-done(((f32[128,32,128]{2,1,0:T(8,128)}), f32[128,32,128]{2,1,0:T(8,128)S(1)}, u32[]{:S(2)}, u32[]{:S(2)}) %all-to-all-start.1) | async-done | bytes 2097184 | tf_op jit(solution)/shard_map/all_to_all | solution.py:305
  61.8 0.0 copy-done
  61.8 20.3 %filtering.1 = f32[4096,128]{1,0:T(8,128)S(1)} custom-call(s32[4]{0:T(128)S(1)} %copy-done.2, f32[128,128]{1,0:T(8,128)S(1)} %bitcast.30, f32[4,64,128]{2,1,0:T(8,128)S(1)} %prepare.1.cl_ref, f32[4096,128]{1,0:T(8,128)S(1)} %bitcast.27, bf16[4,256,8192]{2,1,0:T(8,128)(2,1)} %bitcast.38), custom_call_target="tpu_custom_call" | custom-call | flops 17179869184 | bytes 20971520 | tf_op jit(solution)/shard_map/filtering/pallas_call | solution.py:218
  82.1 34.4 %all_to_all.16 = f32[128,32,128]{2,1,0:T(8,128)S(1)} all-to-all(f32[128,32,128]{2,1,0:T(8,128)S(1)} %bitcast.28), channel_id=1, replica_groups=mesh['hemi'=2,'blk'=64] {'blk','hemi'}, dimensions={0} | all-to-all | bytes 4194304 | tf_op jit(solution)/shard_map/all_to_all | solution.py:307
  116.5 0.2 combine_other.1
  116.6 1.3 %collective-permute-start.2 = (f32[2,64,2,8,128]{4,3,2,1,0:T(8,128)S(1)}, f32[2,64,2,8,128]{4,3,2,1,0:T(8,128)S(1)}, u32[]{:S(2)}, u32[]{:S(2)}) collective-permute-start(f32[2,64,2,8,128]{4,3,2,1,0:T(8,128)S(1)} %combine_other.1), channel_id=1, source_target_pairs={{0,64},{64,0},{1,65},{65,1},{2,66},{66,2},{3,67},{67,3},{4,68},{68... | collective-permute-start | bytes 3145736 | tf_op jit(solution)/shard_map/ppermute | solution.py:309
  118.0 1.1 combine_own.1.whole_ref
  119.1 1.1 collective-permute-done.2.part_ref
  120.3 1.0 place.1
  (1 shorter events, 0.0 us)
Async XLA Ops:
  0.0 22.4 %collective-permute-start = (f32[2,2,64,2,8,128]{5,4,3,2,1,0:T(8,128)}, f32[2,2,64,2,8,128]{5,4,3,2,1,0:T(8,128)}, u32[]{:S(2)}, u32[]{:S(2)}) collective-permute-start(f32[2,2,64,2,8,128]{5,4,3,2,1,0:T(8,128)} %bitcast.33), channel_id=1, source_target_pairs={{0,64},{64,0},{1,65},{65,1},{2,66},{66,2},{3,67},{67,3},{4,68},{68... | collective-permute-start | bytes 6291464 | tf_op jit(solution)/shard_map/ppermute | solution.py:301
  1.4 21.0 %collective-permute-start.1 = (f32[2,2,64,2,8,128]{5,4,3,2,1,0:T(8,128)}, f32[2,2,64,2,8,128]{5,4,3,2,1,0:T(8,128)}, u32[]{:S(2)}, u32[]{:S(2)}) collective-permute-start(f32[2,2,64,2,8,128]{5,4,3,2,1,0:T(8,128)} %bitcast.35), channel_id=1, source_target_pairs={{0,64},{64,0},{1,65},{65,1},{2,66},{66,2},{3,67},{67,3},{4,68},{68... | collective-permute-start | bytes 6291464 | tf_op jit(solution)/shard_map/ppermute | solution.py:302
  26.8 4.8 %copy-start.1 = (f32[16384]{0:T(1024)S(1)}, f32[16384]{0:T(1024)}, u32[]{:S(2)}) copy-start(f32[16384]{0:T(1024)} %param.11) | copy-start | bytes 196612
  26.8 4.8 %copy-start.2 = (s32[4]{0:T(128)S(1)}, s32[4]{0:T(128)}, u32[]{:S(2)}) copy-start(s32[4]{0:T(128)} %m_ref.3) | copy-start | bytes 52
  26.8 35.0 %copy-start = (f32[128,1,128]{2,1,0:T(1,128)S(1)}, f32[128,1,128]{2,1,0:T(1,128)}, u32[]{:S(2)}) copy-start(f32[128,1,128]{2,1,0:T(1,128)} %all_to_all.15) | copy-start | bytes 196612
  26.8 35.0 %all-to-all-start.1 = ((f32[128,32,128]{2,1,0:T(8,128)}), f32[128,32,128]{2,1,0:T(8,128)S(1)}, u32[]{:S(2)}, u32[]{:S(2)}) async-start(f32[128,32,128]{2,1,0:T(8,128)} %bitcast.32), calls=%async_computation.1 | async-start | bytes 4194304 | tf_op jit(solution)/shard_map/all_to_all | solution.py:305
  116.6 3.6 %collective-permute-start.2 = (f32[2,64,2,8,128]{4,3,2,1,0:T(8,128)S(1)}, f32[2,64,2,8,128]{4,3,2,1,0:T(8,128)S(1)}, u32[]{:S(2)}, u32[]{:S(2)}) collective-permute-start(f32[2,64,2,8,128]{4,3,2,1,0:T(8,128)S(1)} %combine_other.1), channel_id=1, source_target_pairs={{0,64},{64,0},{1,65},{65,1},{2,66},{66,2},{3,67},{67,3},{4,68},{68... | collective-permute-start | bytes 3145736 | tf_op jit(solution)/shard_map/ppermute | solution.py:309
where the time goes:
time: 121 us
  blocking collectives  54.7 us (45%)
  waiting for transfers between devices  30.4 us (25%)
  Pallas kernels  27.9 us (23%)
  starting transfers between devices  7.5 us (6%)
    all_to_all x1, blocking collectives, shards(): back = lax.all_to_all(done.reshape(DEV, 32, LANES), ALL, 0, 0, tiled=True)  34.4 us
    all_to_all x1, waiting for transfers between devices, shards(): modes = lax.all_to_all(sums.reshape(DEV, 32, LANES), ALL, 0, 0, tiled=True)  29.2 us
    pallas_call x1, Pallas kernels, filtering(): pl.pallas_call(filter_kernel, in_specs=[smem, vmem, vmem, vmem, hbm], out...  20.3 us
    all_to_all x1, blocking collectives, shards(): all_noise = lax.all_to_all(seen, ALL, 0, 0, tiled=True).reshape(DEV, LANES)  20.3 us
    all_to_all x1, starting transfers between devices, shards(): modes = lax.all_to_all(sums.reshape(DEV, 32, LANES), ALL, 0, 0, tiled=True)  4.78 us
    pallas_call x1, Pallas kernels, messenger(): pl.pallas_call(messenger_kernel, in_specs=[pl.BlockSpec(memory_space=pltp...  4.39 us
  transfers between devices with their start and end apart: 4, of which 2 were waited for; matrix products, arithmetic and copies ran while one was open for 1% of the time, Pallas kernels for 2%

commit v1 on v0

--- a/solution.py
+++ b/solution.py
@@ -5,15 +5,15 @@
 from jax.experimental.pallas import tpu as pltpu
 from jax.sharding import PartitionSpec as P
 
+
 ALL = ("blk", "hemi")
 BLK = 64
 DEV = 128
 SLOTS = 4
 CYCLES = 256
 COLS = 8192
-UNIT = 512
-UNIT_BITS = 9
-SIZES = (4096, 2048, 1024, 512)
+UNIT = 1024
+UNIT_BITS = 10
 LANES = 128
 SWAP = [(0, 1), (1, 0)]
 
@@ -113,8 +113,22 @@
     )(all_noise, weight, data, signal, data2, signal2)
 
 
-def prepare_kernel(m_ref, cl_ref, out_ref, mixed, picked):
+def gram_kernel(m_ref, all_noise_ref, cl_ref, leg_hbm, out_ref, leg, acc, gain, mixed, picked, leg_sem):
     hemi = lax.axis_index("hemi")
+
+    def units_of(slot):
+        return (COLS - ((m_ref[slot] + hemi) >> 1) + UNIT - 1) >> UNIT_BITS
+
+    def fetch(slot, j):
+        cols = pl.ds(pl.multiple_of(j * UNIT, UNIT), UNIT)
+        return pltpu.make_async_copy(leg_hbm.at[slot, :, cols], leg.at[slot, :, cols], leg_sem.at[slot, j])
+
+    for slot in range(SLOTS):
+        @pl.loop(0, units_of(slot))
+        def _(j, slot=slot):
+            fetch(slot, j).start()
+
+    tau = jnp.min(all_noise_ref[...])
     src = lax.broadcasted_iota(jnp.int32, (LANES, LANES), 0)
     dst = lax.broadcasted_iota(jnp.int32, (LANES, LANES), 1)
     pick = jnp.where(src == 2 * (dst & 63) + (dst >> 6), 1.0, 0.0).astype(jnp.float32)
@@ -125,112 +139,81 @@
     picked[...] = jnp.zeros_like(picked)
     picked[0, 0:64, :] = jnp.where(lane < 64, low, pltpu.roll(high, 64, 1))
     picked[1, 0:64, :] = jnp.where(lane < 64, pltpu.roll(low, 64, 1), high)
-    for slot in range(SLOTS):
+
+    @pl.loop(0, SLOTS)
+    def _(slot):
         start = (m_ref[slot] + hemi) >> 1
         parity = (m_ref[slot] + hemi) & 1
         row, turn = start >> 7, start & 127
         back = (LANES - turn) & 127
         here = pltpu.roll(picked[parity, pl.ds(row, 64), :], back, 1)
         after = pltpu.roll(picked[parity, pl.ds(row + 1, 64), :], back, 1)
-        out_ref[slot] = jnp.where(lane < LANES - turn, here, after)
-
-
-def prepare(m_table, cl):
+        cl_cols = jnp.where(lane < LANES - turn, here, after)
+        gain[...] = cl_cols / (cl_cols + tau)
+        acc[...] = jnp.zeros_like(acc)
+
+        @pl.loop(0, units_of(slot))
+        def _(j):
+            fetch(slot, j).wait()
+            table = leg[slot, :, pl.ds(pl.multiple_of(j * UNIT, UNIT), UNIT)]
+            row_of = [gain[pl.ds(j * (UNIT // LANES) + i, 1), :] for i in range(UNIT // LANES)]
+            scaled = (table.astype(jnp.float32) * jnp.concatenate(row_of, axis=1)).astype(jnp.bfloat16)
+            acc[...] += lax.dot_general(scaled, table, (((1,), (1,)), ((), ())), preferred_element_type=jnp.float32)
+
+        whole = acc[...]
+        out_ref[slot, 0] = whole.astype(jnp.bfloat16)
+        out_ref[slot, 1] = (whole - out_ref[slot, 0].astype(jnp.float32)).astype(jnp.bfloat16)
+
+
+def gram(m_table, all_noise, cl, legendre):
     smem = pl.BlockSpec(memory_space=pltpu.SMEM)
     vmem = pl.BlockSpec(memory_space=pltpu.VMEM)
-    return pl.pallas_call(
-        prepare_kernel,
-        in_specs=[smem, vmem],
+    hbm = pl.BlockSpec(memory_space=pltpu.HBM)
+    return pl.pallas_call(
+        gram_kernel,
+        in_specs=[smem, vmem, vmem, hbm],
         out_specs=vmem,
-        out_shape=jax.ShapeDtypeStruct((SLOTS, 64, LANES), jnp.float32),
-        scratch_shapes=[pltpu.VMEM((LANES, LANES), jnp.float32), pltpu.VMEM((2, 136, LANES), jnp.float32)],
-        compiler_params=pltpu.CompilerParams(vmem_limit_bytes=4 << 20),
-        cost_estimate=pl.CostEstimate(flops=4 << 20, bytes_accessed=1 << 18, transcendentals=0),
-        name="prepare",
-    )(m_table, cl)
-
-
-def filter_kernel(m_ref, all_noise_ref, cl_ref, rows_ref, leg_hbm, out_ref, leg, halves, acc, gain, leg_sem):
-    hemi = lax.axis_index("hemi")
+        out_shape=jax.ShapeDtypeStruct((SLOTS, 2, CYCLES, CYCLES), jnp.bfloat16),
+        scratch_shapes=[
+            pltpu.VMEM((SLOTS, CYCLES, COLS), jnp.bfloat16),
+            pltpu.VMEM((CYCLES, CYCLES), jnp.float32),
+            pltpu.VMEM((64, LANES), jnp.float32),
+            pltpu.VMEM((LANES, LANES), jnp.float32),
+            pltpu.VMEM((2, 136, LANES), jnp.float32),
+            pltpu.SemaphoreType.DMA((SLOTS, COLS // UNIT)),
+        ],
+        compiler_params=pltpu.CompilerParams(vmem_limit_bytes=40 << 20),
+        cost_estimate=pl.CostEstimate(flops=4 << 30, bytes_accessed=17 << 20, transcendentals=0),
+        name="gram",
+    )(m_table, all_noise, cl, legendre)
+
+
+def apply_kernel(gram_ref, rows_ref, out_ref, halves):
     stride = 4 * SLOTS
-
-    def units_of(slot):
-        return (COLS - ((m_ref[slot] + hemi) >> 1) + UNIT - 1) >> UNIT_BITS
-
-    def fetch(slot, j):
-        cols = pl.ds(pl.multiple_of(j * UNIT, UNIT), UNIT)
-        return pltpu.make_async_copy(leg_hbm.at[slot, :, cols], leg.at[slot, :, cols], leg_sem.at[slot, j])
-
-    for slot in range(SLOTS):
-        @pl.loop(0, units_of(slot))
-        def _(j, slot=slot):
-            fetch(slot, j).start()
-
-    tau = jnp.min(all_noise_ref[...])
 
     @pl.loop(0, SLOTS)
     def _(slot):
         for q in range(4):
             part = rows_ref[pl.ds(slot * 4 + q, CYCLES, stride=stride), :]
-            halves[slot, q * LANES:(q + 1) * LANES, :] = part.T.astype(jnp.bfloat16)
-
-    def block(slot, at, size):
-        @pl.loop(0, size // UNIT)
-        def _(i):
-            fetch(slot, at + i).wait()
-
-        table = leg[slot, :, pl.ds(pl.multiple_of(at * UNIT, UNIT), size)]
-        coeffs = jnp.dot(halves[slot], table, preferred_element_type=jnp.float32)
-        row_of = [gain[pl.ds(at * (UNIT // LANES) + i, 1), :] for i in range(size // LANES)]
-        filtered = (coeffs * jnp.concatenate(row_of, axis=1)).astype(jnp.bfloat16)
-        acc[...] += lax.dot_general(table, filtered, (((1,), (1,)), ((), ())), preferred_element_type=jnp.float32)
-
-    @pl.loop(0, SLOTS)
-    def _(slot):
-        units = units_of(slot)
-        cl_cols = cl_ref[slot]
-        gain[...] = cl_cols / (cl_cols + tau)
-        acc[...] = jnp.zeros_like(acc)
-        per = SIZES[0] // UNIT
-        whole = units >> (per.bit_length() - 1)
-
-        @pl.loop(0, whole)
-        def _(j):
-            block(slot, j * per, SIZES[0])
-
-        at = whole * per
-        for size in SIZES[1:]:
-            per = size // UNIT
-
-            @pl.when((units & per) != 0)
-            def _(at=at, size=size):
-                block(slot, at, size)
-
-            at = at + (units & per)
+            halves[:, q * LANES:(q + 1) * LANES] = part.astype(jnp.bfloat16)
+        synth = jnp.dot(gram_ref[slot, 0], halves[...], preferred_element_type=jnp.float32)
+        synth = synth + jnp.dot(gram_ref[slot, 1], halves[...], preferred_element_type=jnp.float32)
         for q in range(4):
-            out_ref[pl.ds(slot * 4 + q, CYCLES, stride=stride), :] = acc[:, q * LANES:(q + 1) * LANES]
-
-
-def filtering(m_table, all_noise, cl_cols, rows, legendre):
-    smem = pl.BlockSpec(memory_space=pltpu.SMEM)
+            out_ref[pl.ds(slot * 4 + q, CYCLES, stride=stride), :] = synth[:, q * LANES:(q + 1) * LANES]
+
+
+def apply(grams, rows):
     vmem = pl.BlockSpec(memory_space=pltpu.VMEM)
-    hbm = pl.BlockSpec(memory_space=pltpu.HBM)
-    return pl.pallas_call(
-        filter_kernel,
-        in_specs=[smem, vmem, vmem, vmem, hbm],
+    return pl.pallas_call(
+        apply_kernel,
+        in_specs=[vmem, vmem],
         out_specs=vmem,
         out_shape=jax.ShapeDtypeStruct((CYCLES * 16, LANES), jnp.float32),
-        scratch_shapes=[
-            pltpu.VMEM((SLOTS, CYCLES, COLS), jnp.bfloat16),
-            pltpu.VMEM((SLOTS, 512, CYCLES), jnp.bfloat16),
-            pltpu.VMEM((CYCLES, 512), jnp.float32),
-            pltpu.VMEM((64, LANES), jnp.float32),
-            pltpu.SemaphoreType.DMA((SLOTS, COLS // UNIT)),
-        ],
-        compiler_params=pltpu.CompilerParams(vmem_limit_bytes=44 << 20),
-        cost_estimate=pl.CostEstimate(flops=16 << 30, bytes_accessed=20 << 20, transcendentals=0),
-        name="filtering",
-    )(m_table, all_noise, cl_cols, rows, legendre)
+        scratch_shapes=[pltpu.VMEM((CYCLES, 512), jnp.bfloat16)],
+        compiler_params=pltpu.CompilerParams(vmem_limit_bytes=10 << 20),
+        cost_estimate=pl.CostEstimate(flops=1 << 29, bytes_accessed=5 << 20, transcendentals=0),
+        name="apply",
+    )(grams, rows)
 
 
 def combine_kernel(own, parts, out, *scratch):
@@ -301,9 +284,9 @@
     data2 = lax.ppermute(data, "hemi", SWAP)
     signal2 = lax.ppermute(signal, "hemi", SWAP)
     sums = messenger(all_noise, cycle_weight.reshape(2, LANES), data, signal, data2, signal2)
-    cl_cols = prepare(m_table, cl.reshape(LANES, LANES))
+    grams = gram(m_table, all_noise, cl.reshape(LANES, LANES), legendre.reshape(SLOTS, CYCLES, COLS))
     modes = lax.all_to_all(sums.reshape(DEV, 32, LANES), ALL, 0, 0, tiled=True)
-    done = filtering(m_table, all_noise, cl_cols, modes.reshape(CYCLES * 16, LANES), legendre.reshape(SLOTS, CYCLES, COLS))
+    done = apply(grams, modes.reshape(CYCLES * 16, LANES))
     back = lax.all_to_all(done.reshape(DEV, 32, LANES), ALL, 0, 0, tiled=True)
     parts = back.reshape(BLK, 2, 2, 2, 8, LANES)
     sent = lax.ppermute(combine(parts, False), "hemi", SWAP)

time: 121 us -> 104 us (0.86)
  waiting for transfers between devices: 30.4 us -> 20.8 us
  Pallas kernels: 27.9 us -> 19.6 us
    all_to_all x1, waiting for transfers between devices: 29.2 us -> 19.6 us  [shards(): modes = lax.all_to_all(sums.reshape(DEV, 32, LANES), ALL, 0, 0, tiled=True)]
    pallas_call x2, Pallas kernels: 21.3 us -> 12.9 us  [the longest x1 10.5 us: gram(): pl.pallas_call(gram_kernel, in_specs=[smem, vmem, vmem, hbm], out_specs=v...]
  transfers between devices with their start and end apart: 4 -> 4, of which waited for: 2 -> 2; matrix products, arithmetic and copies ran while one was open for 1% -> 1% of each run, Pallas kernels for 2% -> 11%
where the time goes in v1:
time: 104 us
  blocking collectives  54.9 us (53%)
  waiting for transfers between devices  20.8 us (20%)
  Pallas kernels  19.6 us (19%)
  starting transfers between devices  7.5 us (7%)
    all_to_all x1, blocking collectives, shards(): back = lax.all_to_all(done.reshape(DEV, 32, LANES), ALL, 0, 0, tiled=True)  34.6 us
    all_to_all x1, blocking collectives, shards(): all_noise = lax.all_to_all(seen, ALL, 0, 0, tiled=True).reshape(DEV, LANES)  20.3 us
    all_to_all x1, waiting for transfers between devices, shards(): modes = lax.all_to_all(sums.reshape(DEV, 32, LANES), ALL, 0, 0, tiled=True)  19.6 us
    pallas_call x1, Pallas kernels, gram(): pl.pallas_call(gram_kernel, in_specs=[smem, vmem, vmem, hbm], out_specs=v...  10.5 us
    all_to_all x1, starting transfers between devices, shards(): modes = lax.all_to_all(sums.reshape(DEV, 32, LANES), ALL, 0, 0, tiled=True)  4.78 us
    pallas_call x1, Pallas kernels, messenger(): pl.pallas_call(messenger_kernel, in_specs=[pl.BlockSpec(memory_space=pltp...  4.39 us
    pallas_call x1, Pallas kernels, apply(): pl.pallas_call(apply_kernel, in_specs=[vmem, vmem], out_specs=vmem, out_s...  2.39 us
  transfers between devices with their start and end apart: 4, of which 2 were waited for; matrix products, arithmetic and copies ran while one was open for 1% of the time, Pallas kernels for 11%

profile of v1, /device:TPU:1, one launch (start us, length us, event | category | flops | bytes accessed | tf_op | source)
XLA Modules:
  0.0 103.5 jit_solution(2208897213249912913)
XLA Ops:
  0.0 1.4 %collective-permute-start = (f32[2,2,64,2,8,128]{5,4,3,2,1,0:T(8,128)}, f32[2,2,64,2,8,128]{5,4,3,2,1,0:T(8,128)}, u32[]{:S(2)}, u32[]{:S(2)}) collective-permute-start(f32[2,2,64,2,8,128]{5,4,3,2,1,0:T(8,128)} %bitcast.34), channel_id=1, source_target_pairs={{0,64},{64,0},{1,65},{65,1},{2,66},{66,2},{3,67},{67,3},{4,68},{68... | collective-permute-start | bytes 6291464 | tf_op jit(solution)/shard_map/ppermute | solution.py:284
  1.4 0.0 collective-permute-start.1
  1.4 0.7 pad_bitcast_fusion
  2.1 20.3 %all_to_all.15 = f32[128,1,128]{2,1,0:T(1,128)} all-to-all(f32[128,1,128]{2,1,0:T(1,128)S(1)} %broadcast_in_dim.9), channel_id=1, replica_groups=mesh['hemi'=2,'blk'=64] {'blk','hemi'}, dimensions={0} | all-to-all | bytes 131072 | tf_op jit(solution)/shard_map/all_to_all | solution.py:282
  22.4 0.0 collective-permute-done.data2
  22.4 0.0 collective-permute-done.1.signal2
  22.4 4.4 %messenger.1 = f32[64,2,2,2,8,128]{5,4,3,2,1,0:T(8,128)} custom-call(f32[128,128]{1,0:T(8,128)} %bitcast.29, f32[2,128]{1,0:T(2,128)} %bitcast.38, f32[2,2,64,2,8,128]{5,4,3,2,1,0:T(8,128)} %bitcast.35, f32[2,2,64,2,8,128]{5,4,3,2,1,0:T(8,128)} %bitcast.37, f32[2,2,64,2,8,128]{5,4,3,2,1,0:T(8,128)} %collective-permute-done.data2, ...), custom_call_target="tpu_custom_call" | custom-call | flops 4194304 | bytes 6291456 | tf_op jit(solution)/shard_map/messenger/pallas_call | solution.py:97
  26.8 0.0 copy-start
  26.8 0.0 copy-start.1
  26.8 0.0 copy-start.2
  26.8 4.8 %all-to-all-start.1 = ((f32[128,32,128]{2,1,0:T(8,128)}), f32[128,32,128]{2,1,0:T(8,128)S(1)}, u32[]{:S(2)}, u32[]{:S(2)}) async-start(f32[128,32,128]{2,1,0:T(8,128)} %bitcast.33), calls=%async_computation.1 | async-start | bytes 4194304 | tf_op jit(solution)/shard_map/all_to_all | solution.py:288
  31.6 0.0 copy-done
  31.6 0.0 copy-done.1
  31.6 0.0 copy-done.2
  31.6 10.5 %gram.1.gram_ref = bf16[4,2,256,256]{3,2,1,0:T(8,128)(2,1)S(1)} custom-call(s32[4]{0:T(128)S(1)} %copy-done.2, f32[128,128]{1,0:T(8,128)S(1)} %bitcast.30, f32[128,128]{1,0:T(8,128)S(1)} %bitcast.31, bf16[4,256,8192]{2,1,0:T(8,128)(2,1)} %bitcast.32), custom_call_target="tpu_custom_call" | custom-call | flops 4294967296 | bytes 17825792 | tf_op jit(solution)/shard_map/gram/pallas_call | solution.py:172
  42.1 19.6 %all-to-all-done.1 = f32[128,32,128]{2,1,0:T(8,128)S(1)} async-done(((f32[128,32,128]{2,1,0:T(8,128)}), f32[128,32,128]{2,1,0:T(8,128)S(1)}, u32[]{:S(2)}, u32[]{:S(2)}) %all-to-all-start.1) | async-done | bytes 2097184 | tf_op jit(solution)/shard_map/all_to_all | solution.py:288
  61.8 2.4 %apply.1 = f32[4096,128]{1,0:T(8,128)S(1)} custom-call(bf16[4,2,256,256]{3,2,1,0:T(8,128)(2,1)S(1)} %gram.1.gram_ref, f32[4096,128]{1,0:T(8,128)S(1)} %bitcast.27), custom_call_target="tpu_custom_call" | custom-call | flops 536870912 | bytes 5242880 | tf_op jit(solution)/shard_map/apply/pallas_call | solution.py:207
  64.2 34.6 %all_to_all.16 = f32[128,32,128]{2,1,0:T(8,128)S(1)} all-to-all(f32[128,32,128]{2,1,0:T(8,128)S(1)} %bitcast.28), channel_id=1, replica_groups=mesh['hemi'=2,'blk'=64] {'blk','hemi'}, dimensions={0} | all-to-all | bytes 4194304 | tf_op jit(solution)/shard_map/all_to_all | solution.py:290
  98.8 0.2 combine_other.1
  98.9 1.3 %collective-permute-start.2 = (f32[2,64,2,8,128]{4,3,2,1,0:T(8,128)S(1)}, f32[2,64,2,8,128]{4,3,2,1,0:T(8,128)S(1)}, u32[]{:S(2)}, u32[]{:S(2)}) collective-permute-start(f32[2,64,2,8,128]{4,3,2,1,0:T(8,128)S(1)} %combine_other.1), channel_id=1, source_target_pairs={{0,64},{64,0},{1,65},{65,1},{2,66},{66,2},{3,67},{67,3},{4,68},{68... | collective-permute-start | bytes 3145736 | tf_op jit(solution)/shard_map/ppermute | solution.py:292
  100.3 1.1 %combine_own.1.whole_ref = f32[2,2,64,2,8,128]{5,4,3,2,1,0:T(8,128)} custom-call(f32[64,2,2,2,8,128]{5,4,3,2,1,0:T(8,128)S(1)} %bitcast.26), custom_call_target="tpu_custom_call" | custom-call | flops 1048576 | bytes 3145728 | tf_op jit(solution)/shard_map/combine_own/pallas_call | solution.py:247
  101.4 1.1 %collective-permute-done.2.part_ref = f32[2,64,2,8,128]{4,3,2,1,0:T(8,128)S(1)} collective-permute-done((f32[2,64,2,8,128]{4,3,2,1,0:T(8,128)S(1)}, f32[2,64,2,8,128]{4,3,2,1,0:T(8,128)S(1)}, u32[]{:S(2)}, u32[]{:S(2)}) %collective-permute-start.2) | collective-permute-done | bytes 1048608 | tf_op jit(solution)/shard_map/ppermute | solution.py:292
  102.6 1.0 place.1
  (1 shorter events, 0.0 us)
Async XLA Ops:
  0.0 22.4 %collective-permute-start = (f32[2,2,64,2,8,128]{5,4,3,2,1,0:T(8,128)}, f32[2,2,64,2,8,128]{5,4,3,2,1,0:T(8,128)}, u32[]{:S(2)}, u32[]{:S(2)}) collective-permute-start(f32[2,2,64,2,8,128]{5,4,3,2,1,0:T(8,128)} %bitcast.34), channel_id=1, source_target_pairs={{0,64},{64,0},{1,65},{65,1},{2,66},{66,2},{3,67},{67,3},{4,68},{68... | collective-permute-start | bytes 6291464 | tf_op jit(solution)/shard_map/ppermute | solution.py:284
  1.4 21.0 %collective-permute-start.1 = (f32[2,2,64,2,8,128]{5,4,3,2,1,0:T(8,128)}, f32[2,2,64,2,8,128]{5,4,3,2,1,0:T(8,128)}, u32[]{:S(2)}, u32[]{:S(2)}) collective-permute-start(f32[2,2,64,2,8,128]{5,4,3,2,1,0:T(8,128)} %bitcast.36), channel_id=1, source_target_pairs={{0,64},{64,0},{1,65},{65,1},{2,66},{66,2},{3,67},{67,3},{4,68},{68... | collective-permute-start | bytes 6291464 | tf_op jit(solution)/shard_map/ppermute | solution.py:285
  26.8 4.8 %copy-start = (f32[128,1,128]{2,1,0:T(1,128)S(1)}, f32[128,1,128]{2,1,0:T(1,128)}, u32[]{:S(2)}) copy-start(f32[128,1,128]{2,1,0:T(1,128)} %all_to_all.15) | copy-start | bytes 196612
  26.8 4.8 %copy-start.1 = (f32[16384]{0:T(1024)S(1)}, f32[16384]{0:T(1024)}, u32[]{:S(2)}) copy-start(f32[16384]{0:T(1024)} %param.11) | copy-start | bytes 196612
  26.8 4.8 %copy-start.2 = (s32[4]{0:T(128)S(1)}, s32[4]{0:T(128)}, u32[]{:S(2)}) copy-start(s32[4]{0:T(128)} %m_ref.1) | copy-start | bytes 52
  26.8 35.0 %all-to-all-start.1 = ((f32[128,32,128]{2,1,0:T(8,128)}), f32[128,32,128]{2,1,0:T(8,128)S(1)}, u32[]{:S(2)}, u32[]{:S(2)}) async-start(f32[128,32,128]{2,1,0:T(8,128)} %bitcast.33), calls=%async_computation.1 | async-start | bytes 4194304 | tf_op jit(solution)/shard_map/all_to_all | solution.py:288
  98.9 3.6 %collective-permute-start.2 = (f32[2,64,2,8,128]{4,3,2,1,0:T(8,128)S(1)}, f32[2,64,2,8,128]{4,3,2,1,0:T(8,128)S(1)}, u32[]{:S(2)}, u32[]{:S(2)}) collective-permute-start(f32[2,64,2,8,128]{4,3,2,1,0:T(8,128)S(1)} %combine_other.1), channel_id=1, source_target_pairs={{0,64},{64,0},{1,65},{65,1},{2,66},{66,2},{3,67},{67,3},{4,68},{68... | collective-permute-start | bytes 3145736 | tf_op jit(solution)/shard_map/ppermute | solution.py:292

commit v2 on v1

v2 whole, which is shorter than its diff:
```python
import jax
import jax.numpy as jnp
from jax import lax
from jax.experimental import pallas as pl
from jax.experimental.pallas import tpu as pltpu
from jax.sharding import PartitionSpec as P


ALL = ("hemi", "blk")
BLK = 64
DEV = 128
SLOTS = 4
CYCLES = 256
COLS = 8192
UNIT = 1024
UNIT_BITS = 10
LANES = 128
SWAP = [(0, 1), (1, 0)]


def to_tiles(array):
    array = array.reshape(4, 256, 2, 2, LANES).transpose(0, 1, 3, 2, 4)
    return array.reshape(4, BLK, 2, 8, LANES)


def from_tiles(array):
    return array.reshape(4, 256, 2, 2, LANES).transpose(0, 1, 3, 2, 4).reshape(1, 4, 256, 2, 256)


BIG = 3e38
VMEM_ALL = 67043328


STAGES = 8


def messenger_kernel(all_noise_ref, weight_hbm, data, signal, out, ins, sums, weights, in_sem, out_sem, weight_sem):
    blk = lax.axis_index("blk")
    me = lax.axis_index("hemi") * BLK + blk
    step = BLK // STAGES
    sources = (data, signal)

    def fetch(n, i):
        at = pl.ds(i * step, step)
        return pltpu.make_async_copy(sources[n].at[:, at], ins.at[n, :, at], in_sem.at[n, i])

    def store(i):
        at = pl.ds(i * step, step)
        return pltpu.make_async_copy(sums.at[:, at], out.at[:, at], out_sem.at[i])

    weight_copy = pltpu.make_async_copy(weight_hbm, weights, weight_sem)
    weight_copy.start()
    for i in range(STAGES):
        for n in range(2):
            fetch(n, i).start()
    tau = jnp.min(all_noise_ref[...])
    lane = lax.broadcasted_iota(jnp.int32, (1, LANES), 1)
    own_row = all_noise_ref[pl.ds(me, 1), :]

    def pick(row, at):
        return jnp.sum(jnp.where(lane == at, row, 0.0), axis=1, keepdims=True)

    coefs = []
    weight_copy.wait()
    weight_row = weights[pl.ds((4 * blk) >> 7, 1), :]
    for r in range(4):
        n = pick(own_row, r)
        scale = pick(weight_row, ((4 * blk) & 127) + r) / n
        coefs.append((jnp.broadcast_to(scale * tau, (8, LANES)), jnp.broadcast_to(scale * (n - tau), (8, LANES))))
    small = 4
    for i in range(STAGES):
        for n in range(2):
            fetch(n, i).wait()

        @pl.loop(0, step // small)
        def _(j, i=i):
            at = pl.ds(i * step + j * small, small)
            for r in range(4):
                a, b = coefs[r]
                for pair in range(2):
                    sums[pair, at, r] = a * ins[0, r, at, pair] + b * ins[1, r, at, pair]

        store(i).start()
    for i in range(STAGES):
        store(i).wait()


def messenger(all_noise, weight, data, signal):
    hbm = pl.BlockSpec(memory_space=pltpu.HBM)
    return pl.pallas_call(
        messenger_kernel,
        in_specs=[pl.BlockSpec(memory_space=pltpu.VMEM)] + [hbm] * 3,
        out_specs=hbm,
        out_shape=jax.ShapeDtypeStruct((2, BLK, 4, 8, LANES), jnp.float32),
        scratch_shapes=[
            pltpu.VMEM((2, 4, BLK, 2, 8, LANES), jnp.float32),
            pltpu.VMEM((2, BLK, 4, 8, LANES), jnp.float32),
            pltpu.VMEM((2, LANES), jnp.float32),
            pltpu.SemaphoreType.DMA((2, STAGES)),
            pltpu.SemaphoreType.DMA((STAGES,)),
            pltpu.SemaphoreType.DMA,
        ],
        compiler_params=pltpu.CompilerParams(vmem_limit_bytes=VMEM_ALL),
        cost_estimate=pl.CostEstimate(flops=4 << 20, bytes_accessed=6 << 20, transcendentals=0),
        name="messenger",
    )(all_noise, weight, data, signal)


def gram_kernel(m_ref, all_noise_ref, cl_ref, leg_hbm, out_ref, leg, acc, gain, mixed, picked, leg_sem):
    hemi = lax.axis_index("hemi")

    def units_of(slot):
        return (COLS - ((m_ref[slot] + hemi) >> 1) + UNIT - 1) >> UNIT_BITS

    def fetch(slot, j):
        cols = pl.ds(pl.multiple_of(j * UNIT, UNIT), UNIT)
        return pltpu.make_async_copy(leg_hbm.at[slot, :, cols], leg.at[slot, :, cols], leg_sem.at[slot, j])

    for slot in range(SLOTS):
        @pl.loop(0, units_of(slot))
        def _(j, slot=slot):
            fetch(slot, j).start()

    tau = jnp.min(all_noise_ref[...])
    src = lax.broadcasted_iota(jnp.int32, (LANES, LANES), 0)
    dst = lax.broadcasted_iota(jnp.int32, (LANES, LANES), 1)
    pick = jnp.where(src == 2 * (dst & 63) + (dst >> 6), 1.0, 0.0).astype(jnp.float32)
    mixed[...] = jnp.dot(cl_ref[...], pick, precision=lax.Precision.HIGHEST, preferred_element_type=jnp.float32)
    low = mixed[pl.ds(0, 64, stride=2), :]
    high = mixed[pl.ds(1, 64, stride=2), :]
    lane = lax.broadcasted_iota(jnp.int32, (64, LANES), 1)
    picked[...] = jnp.zeros_like(picked)
    picked[0, 0:64, :] = jnp.where(lane < 64, low, pltpu.roll(high, 64, 1))
    picked[1, 0:64, :] = jnp.where(lane < 64, pltpu.roll(low, 64, 1), high)

    @pl.loop(0, SLOTS)
    def _(slot):
        start = (m_ref[slot] + hemi) >> 1
        parity = (m_ref[slot] + hemi) & 1
        row, turn = start >> 7, start & 127
        back = (LANES - turn) & 127
        here = pltpu.roll(picked[parity, pl.ds(row, 64), :], back, 1)
        after = pltpu.roll(picked[parity, pl.ds(row + 1, 64), :], back, 1)
        cl_cols = jnp.where(lane < LANES - turn, here, after)
        gain[...] = cl_cols / (cl_cols + tau)
        acc[...] = jnp.zeros_like(acc)

        @pl.loop(0, units_of(slot))
        def _(j):
            fetch(slot, j).wait()
            table = leg[slot, :, pl.ds(pl.multiple_of(j * UNIT, UNIT), UNIT)]
            row_of = [gain[pl.ds(j * (UNIT // LANES) + i, 1), :] for i in range(UNIT // LANES)]
            scaled = (table.astype(jnp.float32) * jnp.concatenate(row_of, axis=1)).astype(jnp.bfloat16)
            acc[...] += lax.dot_general(scaled, table, (((1,), (1,)), ((), ())), preferred_element_type=jnp.float32)

        out_ref[slot >> 1, slot & 1] = acc[...]


def gram(m_table, all_noise, cl, legendre):
    smem = pl.BlockSpec(memory_space=pltpu.SMEM)
    vmem = pl.BlockSpec(memory_space=pltpu.VMEM)
    hbm = pl.BlockSpec(memory_space=pltpu.HBM)
    return pl.pallas_call(
        gram_kernel,
        in_specs=[smem, vmem, vmem, hbm],
        out_specs=vmem,
        out_shape=jax.ShapeDtypeStruct((2, 2, CYCLES, CYCLES), jnp.float32),
        scratch_shapes=[
            pltpu.VMEM((SLOTS, CYCLES, COLS), jnp.bfloat16),
            pltpu.VMEM((CYCLES, CYCLES), jnp.float32),
            pltpu.VMEM((64, LANES), jnp.float32),
            pltpu.VMEM((LANES, LANES), jnp.float32),
            pltpu.VMEM((2, 136, LANES), jnp.float32),
            pltpu.SemaphoreType.DMA((SLOTS, COLS // UNIT)),
        ],
        compiler_params=pltpu.CompilerParams(vmem_limit_bytes=40 << 20),
        cost_estimate=pl.CostEstimate(flops=4 << 30, bytes_accessed=17 << 20, transcendentals=0),
        name="gram",
    )(m_table, all_noise, cl, legendre)


def arrange_kernel(own_ref, other_ref, out_ref):
    hemi = lax.axis_index("hemi")
    for slot in range(2):
        for parity in range(2):
            whole = jnp.where(hemi == parity, own_ref[hemi, slot], other_ref[hemi, slot])
            near = whole.astype(jnp.bfloat16)
            out_ref[slot, parity, 0] = near
            out_ref[slot, parity, 1] = (whole - near.astype(jnp.float32)).astype(jnp.bfloat16)


def arrange(own, other):
    vmem = pl.BlockSpec(memory_space=pltpu.VMEM)
    return pl.pallas_call(
        arrange_kernel,
        in_specs=[vmem, vmem],
        out_specs=vmem,
        out_shape=jax.ShapeDtypeStruct((2, 2, 2, CYCLES, CYCLES), jnp.bfloat16),
        compiler_params=pltpu.CompilerParams(vmem_limit_bytes=8 << 20),
        cost_estimate=pl.CostEstimate(flops=1 << 20, bytes_accessed=3 << 20, transcendentals=0),
        name="arrange",
    )(own, other)


def apply_kernel(matrix_ref, rows_ref, out_ref, halves):
    south = CYCLES * 8
    for slot in range(2):
        for q in range(4):
            at = slot * 4 + q
            first = rows_ref[pl.ds(at, CYCLES, stride=8), :]
            second = rows_ref[pl.ds(south + at, CYCLES, stride=8), :]
            halves[slot, 0, :, q * LANES:(q + 1) * LANES] = (first + second).astype(jnp.bfloat16)
            halves[slot, 1, :, q * LANES:(q + 1) * LANES] = (first - second).astype(jnp.bfloat16)
    for slot in range(2):
        synth = []
        for parity in range(2):
            synth.append(
                jnp.dot(matrix_ref[slot, parity, 0], halves[slot, parity], preferred_element_type=jnp.float32)
                + jnp.dot(matrix_ref[slot, parity, 1], halves[slot, parity], preferred_element_type=jnp.float32)
            )
        for q in range(4):
            at = slot * 4 + q
            even, odd = synth[0][:, q * LANES:(q + 1) * LANES], synth[1][:, q * LANES:(q + 1) * LANES]
            out_ref[pl.ds(at, CYCLES, stride=8), :] = even + odd
            out_ref[pl.ds(south + at, CYCLES, stride=8), :] = even - odd


def apply(matrices, rows):
    vmem = pl.BlockSpec(memory_space=pltpu.VMEM)
    return pl.pallas_call(
        apply_kernel,
        in_specs=[vmem, vmem],
        out_specs=vmem,
        out_shape=jax.ShapeDtypeStruct((CYCLES * 16, LANES), jnp.float32),
        scratch_shapes=[pltpu.VMEM((2, 2, CYCLES, 512), jnp.bfloat16)],
        compiler_params=pltpu.CompilerParams(vmem_limit_bytes=12 << 20),
        cost_estimate=pl.CostEstimate(flops=1 << 29, bytes_accessed=6 << 20, transcendentals=0),
        name="apply",
    )(matrices, rows)


def place_kernel(parts, out, sem):
    copies = [
        pltpu.make_async_copy(parts.at[pair, :, r], out.at[r, :, pair], sem.at[pair, r]) for pair in range(2) for r in range(4)
    ]
    for copy in copies:
        copy.start()
    for copy in copies:
        copy.wait()


def place(parts):
    return pl.pallas_call(
        place_kernel,
        in_specs=[pl.BlockSpec(memory_space=pltpu.VMEM)],
        out_specs=pl.BlockSpec(memory_space=pltpu.HBM),
        out_shape=jax.ShapeDtypeStruct((4, BLK, 2, 8, LANES), jnp.float32),
        scratch_shapes=[pltpu.SemaphoreType.DMA((2, 4))],
        compiler_params=pltpu.CompilerParams(vmem_limit_bytes=4 << 20),
        cost_estimate=pl.CostEstimate(flops=0, bytes_accessed=4 << 20, transcendentals=0),
        name="place",
    )(parts)


def shards(data, signal, noise, cycle_weight, cl, legendre, m_table):
    seen = jnp.broadcast_to(jnp.pad(noise, ((0, 0), (0, LANES - 4)), constant_values=BIG)[None], (DEV, 1, LANES))
    all_noise = lax.all_to_all(seen, ALL, 0, 0, tiled=True).reshape(DEV, LANES)
    sums = messenger(all_noise, cycle_weight.reshape(2, LANES), to_tiles(data), to_tiles(signal))
    own = gram(m_table, all_noise, cl.reshape(LANES, LANES), legendre.reshape(SLOTS, CYCLES, COLS))
    modes = lax.all_to_all(sums.reshape(DEV, 32, LANES), ALL, 0, 0, tiled=True)
    other = lax.ppermute(own, "hemi", SWAP)
    matrices = arrange(own, other)
    done = apply(matrices, modes.reshape(CYCLES * 16, LANES))
    back = lax.all_to_all(done.reshape(DEV, 32, LANES), ALL, 0, 0, tiled=True)
    return from_tiles(place(back.reshape(2, BLK, 4, 8, LANES)))


def solution(mesh):
    return jax.shard_map(
        shards,
        mesh=mesh,
        in_specs=(
            P("hemi", "blk", None, None, None),
            P("hemi", "blk", None, None, None),
            P("hemi", "blk"),
            P(),
            P(),
            P("blk", "hemi", None, None),
            P("blk"),
        ),
        out_specs=P("hemi", "blk", None, None, None),
        check_vma=False,
    )
```

time: 104 us -> 99.9 us (0.961)
  waiting for transfers between devices: 20.8 us -> 18.3 us
  blocking collectives: 54.9 us -> 57.3 us
  Pallas kernels: 19.6 us -> 17.6 us
  starting transfers between devices: 7.5 us -> 5.51 us
    all_to_all x1, waiting for transfers between devices: 19.6 us -> 16 us  [shards(): modes = lax.all_to_all(sums.reshape(DEV, 32, LANES), ALL, 0, 0, tiled=True)]
    ppermute x3 -> x1, starting transfers between devices: 2.72 us -> 1.16 us  [shards(): other = lax.ppermute(own, 'hemi', SWAP)]
    all_to_all x1, blocking collectives: 34.6 us -> 36.1 us  [shards(): back = lax.all_to_all(done.reshape(DEV, 32, LANES), ALL, 0, 0, tiled=True)]
    ppermute x3 -> x1, waiting for transfers between devices: 1.15 us -> 2.29 us  [shards(): other = lax.ppermute(own, 'hemi', SWAP)]
    pallas_call x1, Pallas kernels: 2.39 us -> 1.31 us  [apply(): pl.pallas_call(apply_kernel, in_specs=[vmem, vmem], out_specs=vmem, out_s...]
    pallas_call x2 -> x1, Pallas kernels: 1.29 us -> 0.23 us  [arrange(): pl.pallas_call(arrange_kernel, in_specs=[vmem, vmem], out_specs=vmem, out...]
  transfers between devices with their start and end apart: 4 -> 2, of which waited for: 2 -> 2; matrix products, arithmetic and copies ran while one was open for 1% -> 0% of each run, Pallas kernels for 11% -> 11%
where the time goes in v2:
time: 99.9 us; the launch traced here: 99.6 us
  blocking collectives  57.3 us (57%)
  waiting for transfers between devices  18.3 us (18%)
  Pallas kernels  17.6 us (18%)
  starting transfers between devices  5.51 us (6%)
    all_to_all x1, blocking collectives, shards(): back = lax.all_to_all(done.reshape(DEV, 32, LANES), ALL, 0, 0, tiled=True)  36.1 us
    all_to_all x1, blocking collectives, shards(): all_noise = lax.all_to_all(seen, ALL, 0, 0, tiled=True).reshape(DEV, LANES)  21.2 us
    all_to_all x1, waiting for transfers between devices, shards(): modes = lax.all_to_all(sums.reshape(DEV, 32, LANES), ALL, 0, 0, tiled=True)  16 us
    pallas_call x1, Pallas kernels, gram(): pl.pallas_call(gram_kernel, in_specs=[smem, vmem, vmem, hbm], out_specs=v...  10.3 us
    all_to_all x1, starting transfers between devices, shards(): modes = lax.all_to_all(sums.reshape(DEV, 32, LANES), ALL, 0, 0, tiled=True)  4.36 us
    pallas_call x1, Pallas kernels, messenger(): pl.pallas_call(messenger_kernel, in_specs=[pl.BlockSpec(memory_space=pltp...  4.35 us
    ppermute x1, waiting for transfers between devices, shards(): other = lax.ppermute(own, 'hemi', SWAP)  2.29 us
  transfers between devices with their start and end apart: 2, of which 2 were waited for; matrix products, arithmetic and copies ran while one was open for 0% of the time, Pallas kernels for 11%

profile of v2, /device:TPU:1, one launch (start us, length us, event | category | flops | bytes accessed | tf_op | source)
XLA Modules:
  0.0 99.6 jit_solution(16226579140773329605)
XLA Ops:
  0.0 0.7 pad_bitcast_fusion
  0.7 21.2 %all_to_all.15 = f32[128,1,128]{2,1,0:T(1,128)} all-to-all(f32[128,1,128]{2,1,0:T(1,128)S(1)} %broadcast_in_dim.9), channel_id=1, replica_groups=mesh['hemi'=2,'blk'=64] {'hemi','blk'}, dimensions={0} | all-to-all | bytes 131072 | tf_op jit(solution)/shard_map/all_to_all | solution.py:267
  21.9 4.3 %messenger.1 = f32[2,64,4,8,128]{4,3,2,1,0:T(8,128)} custom-call(f32[128,128]{1,0:T(8,128)} %bitcast.28, f32[2,128]{1,0:T(2,128)} %bitcast.35, f32[4,64,2,8,128]{4,3,2,1,0:T(8,128)} %bitcast.33, f32[4,64,2,8,128]{4,3,2,1,0:T(8,128)} %bitcast.34), custom_call_target="tpu_custom_call" | custom-call | flops 4194304 | bytes 6291456 | tf_op jit(solution)/shard_map/messenger/pallas_call | solution.py:90
  26.3 0.0 copy-start
  26.3 0.0 copy-start.1
  26.3 0.0 copy-start.2
  26.3 4.4 %all-to-all-start.1 = ((f32[128,32,128]{2,1,0:T(8,128)}), f32[128,32,128]{2,1,0:T(8,128)S(1)}, u32[]{:S(2)}, u32[]{:S(2)}) async-start(f32[128,32,128]{2,1,0:T(8,128)} %bitcast.32), calls=%async_computation.1 | async-start | bytes 4194304 | tf_op jit(solution)/shard_map/all_to_all | solution.py:270
  30.7 0.0 copy-done
  30.7 0.0 copy-done.1
  30.7 0.0 copy-done.2
  30.7 10.3 %gram.1.own_ref = f32[2,2,256,256]{3,2,1,0:T(8,128)S(1)} custom-call(s32[4]{0:T(128)S(1)} %copy-done.2, f32[128,128]{1,0:T(8,128)S(1)} %bitcast.29, f32[128,128]{1,0:T(8,128)S(1)} %bitcast.30, bf16[4,256,8192]{2,1,0:T(8,128)(2,1)} %bitcast.31), custom_call_target="tpu_custom_call" | custom-call | flops 4294967296 | bytes 17825792 | tf_op jit(solution)/shard_map/gram/pallas_call | solution.py:163
  41.1 1.2 %collective-permute-start = (f32[2,2,256,256]{3,2,1,0:T(8,128)S(1)}, f32[2,2,256,256]{3,2,1,0:T(8,128)S(1)}, u32[]{:S(2)}, u32[]{:S(2)}) collective-permute-start(f32[2,2,256,256]{3,2,1,0:T(8,128)S(1)} %gram.1.own_ref), channel_id=1, source_target_pairs={{0,64},{64,0},{1,65},{65,1},{2,66},{66,2},{3,67},{67,3},{4,68},{68... | collective-permute-start | bytes 3145736 | tf_op jit(solution)/shard_map/ppermute | solution.py:271
  42.2 2.3 %collective-permute-done.other_ref = f32[2,2,256,256]{3,2,1,0:T(8,128)S(1)} collective-permute-done((f32[2,2,256,256]{3,2,1,0:T(8,128)S(1)}, f32[2,2,256,256]{3,2,1,0:T(8,128)S(1)}, u32[]{:S(2)}, u32[]{:S(2)}) %collective-permute-start) | collective-permute-done | bytes 1048608 | tf_op jit(solution)/shard_map/ppermute | solution.py:271
  44.5 0.2 arrange.1.matrix_ref
  44.7 16.0 %all-to-all-done.1 = f32[128,32,128]{2,1,0:T(8,128)S(1)} async-done(((f32[128,32,128]{2,1,0:T(8,128)}), f32[128,32,128]{2,1,0:T(8,128)S(1)}, u32[]{:S(2)}, u32[]{:S(2)}) %all-to-all-start.1) | async-done | bytes 2097184 | tf_op jit(solution)/shard_map/all_to_all | solution.py:270
  60.8 1.3 %apply.1 = f32[4096,128]{1,0:T(8,128)S(1)} custom-call(bf16[2,2,2,256,256]{4,3,2,1,0:T(8,128)(2,1)S(1)} %arrange.1.matrix_ref, f32[4096,128]{1,0:T(8,128)S(1)} %bitcast.25), custom_call_target="tpu_custom_call" | custom-call | flops 536870912 | bytes 6291456 | tf_op jit(solution)/shard_map/apply/pallas_call | solution.py:230
  62.1 36.1 %all_to_all.16 = f32[128,32,128]{2,1,0:T(8,128)S(1)} all-to-all(f32[128,32,128]{2,1,0:T(8,128)S(1)} %bitcast.26), channel_id=1, replica_groups=mesh['hemi'=2,'blk'=64] {'hemi','blk'}, dimensions={0} | all-to-all | bytes 4194304 | tf_op jit(solution)/shard_map/all_to_all | solution.py:274
  98.2 1.4 %place.1 = f32[4,64,2,8,128]{4,3,2,1,0:T(8,128)} custom-call(f32[2,64,4,8,128]{4,3,2,1,0:T(8,128)S(1)} %bitcast.27), custom_call_target="tpu_custom_call" | custom-call | bytes 4194304 | tf_op jit(solution)/shard_map/place/pallas_call | solution.py:253
  (1 shorter events, 0.0 us)
Async XLA Ops:
  26.3 4.4 %copy-start = (f32[128,1,128]{2,1,0:T(1,128)S(1)}, f32[128,1,128]{2,1,0:T(1,128)}, u32[]{:S(2)}) copy-start(f32[128,1,128]{2,1,0:T(1,128)} %all_to_all.15) | copy-start | bytes 196612
  26.3 4.4 %copy-start.1 = (f32[16384]{0:T(1024)S(1)}, f32[16384]{0:T(1024)}, u32[]{:S(2)}) copy-start(f32[16384]{0:T(1024)} %param.11) | copy-start | bytes 196612
  26.3 4.4 %copy-start.2 = (s32[4]{0:T(128)S(1)}, s32[4]{0:T(128)}, u32[]{:S(2)}) copy-start(s32[4]{0:T(128)} %m_ref.1) | copy-start | bytes 52
  26.3 34.5 %all-to-all-start.1 = ((f32[128,32,128]{2,1,0:T(8,128)}), f32[128,32,128]{2,1,0:T(8,128)S(1)}, u32[]{:S(2)}, u32[]{:S(2)}) async-start(f32[128,32,128]{2,1,0:T(8,128)} %bitcast.32), calls=%async_computation.1 | async-start | bytes 4194304 | tf_op jit(solution)/shard_map/all_to_all | solution.py:270
  41.1 3.4 %collective-permute-start = (f32[2,2,256,256]{3,2,1,0:T(8,128)S(1)}, f32[2,2,256,256]{3,2,1,0:T(8,128)S(1)}, u32[]{:S(2)}, u32[]{:S(2)}) collective-permute-start(f32[2,2,256,256]{3,2,1,0:T(8,128)S(1)} %gram.1.own_ref), channel_id=1, source_target_pairs={{0,64},{64,0},{1,65},{65,1},{2,66},{66,2},{3,67},{67,3},{4,68},{68... | collective-permute-start | bytes 3145736 | tf_op jit(solution)/shard_map/ppermute | solution.py:271

commit v3 on v2

--- a/solution.py
+++ b/solution.py
@@ -31,10 +31,10 @@
 VMEM_ALL = 67043328
 
 
-STAGES = 8
-
-
-def messenger_kernel(all_noise_ref, weight_hbm, data, signal, out, ins, sums, weights, in_sem, out_sem, weight_sem):
+STAGES = 4
+
+
+def messenger_kernel(noise_hbm, weight_hbm, data, signal, out, ins, sums, weights, all_noise, in_sem, out_sem, small_sem):
     blk = lax.axis_index("blk")
     me = lax.axis_index("hemi") * BLK + blk
     step = BLK // STAGES
@@ -48,14 +48,17 @@
         at = pl.ds(i * step, step)
         return pltpu.make_async_copy(sums.at[:, at], out.at[:, at], out_sem.at[i])
 
-    weight_copy = pltpu.make_async_copy(weight_hbm, weights, weight_sem)
+    noise_copy = pltpu.make_async_copy(noise_hbm, all_noise, small_sem.at[0])
+    weight_copy = pltpu.make_async_copy(weight_hbm, weights, small_sem.at[1])
+    noise_copy.start()
     weight_copy.start()
     for i in range(STAGES):
         for n in range(2):
             fetch(n, i).start()
-    tau = jnp.min(all_noise_ref[...])
     lane = lax.broadcasted_iota(jnp.int32, (1, LANES), 1)
-    own_row = all_noise_ref[pl.ds(me, 1), :]
+    noise_copy.wait()
+    tau = jnp.min(all_noise[...])
+    own_row = all_noise[pl.ds(me, 1), :]
 
     def pick(row, at):
         return jnp.sum(jnp.where(lane == at, row, 0.0), axis=1, keepdims=True)
@@ -89,16 +92,17 @@
     hbm = pl.BlockSpec(memory_space=pltpu.HBM)
     return pl.pallas_call(
         messenger_kernel,
-        in_specs=[pl.BlockSpec(memory_space=pltpu.VMEM)] + [hbm] * 3,
+        in_specs=[hbm] * 4,
         out_specs=hbm,
         out_shape=jax.ShapeDtypeStruct((2, BLK, 4, 8, LANES), jnp.float32),
         scratch_shapes=[
             pltpu.VMEM((2, 4, BLK, 2, 8, LANES), jnp.float32),
             pltpu.VMEM((2, BLK, 4, 8, LANES), jnp.float32),
             pltpu.VMEM((2, LANES), jnp.float32),
+            pltpu.VMEM((DEV, LANES), jnp.float32),
             pltpu.SemaphoreType.DMA((2, STAGES)),
             pltpu.SemaphoreType.DMA((STAGES,)),
-            pltpu.SemaphoreType.DMA,
+            pltpu.SemaphoreType.DMA((2,)),
         ],
         compiler_params=pltpu.CompilerParams(vmem_limit_bytes=VMEM_ALL),
         cost_estimate=pl.CostEstimate(flops=4 << 20, bytes_accessed=6 << 20, transcendentals=0),

time: 99.9 us -> 99 us (level)
  no operation moved by 1% of the time
where the time goes in v3:
time: 99 us; the launch traced here: 98.7 us
  blocking collectives  57.3 us (58%)
  waiting for transfers between devices  18.3 us (18%)
  Pallas kernels  16.8 us (17%)
  starting transfers between devices  5.51 us (6%)
    all_to_all x1, blocking collectives, shards(): back = lax.all_to_all(done.reshape(DEV, 32, LANES), ALL, 0, 0, tiled=True)  36.1 us
    all_to_all x1, blocking collectives, shards(): all_noise = lax.all_to_all(seen, ALL, 0, 0, tiled=True).reshape(DEV, LANES)  21.2 us
    all_to_all x1, waiting for transfers between devices, shards(): modes = lax.all_to_all(sums.reshape(DEV, 32, LANES), ALL, 0, 0, tiled=True)  16 us
    pallas_call x1, Pallas kernels, gram(): pl.pallas_call(gram_kernel, in_specs=[smem, vmem, vmem, hbm], out_specs=v...  10.4 us
    all_to_all x1, starting transfers between devices, shards(): modes = lax.all_to_all(sums.reshape(DEV, 32, LANES), ALL, 0, 0, tiled=True)  4.36 us
    pallas_call x1, Pallas kernels, messenger(): pl.pallas_call(messenger_kernel, in_specs=[hbm] * 4, out_specs=hbm, out_s...  3.5 us
    ppermute x1, waiting for transfers between devices, shards(): other = lax.ppermute(own, 'hemi', SWAP)  2.29 us
  transfers between devices with their start and end apart: 2, of which 2 were waited for; matrix products, arithmetic and copies ran while one was open for 0% of the time, Pallas kernels for 11%

profile of v3, /device:TPU:1, one launch (start us, length us, event | category | flops | bytes accessed | tf_op | source)
XLA Modules:
  0.0 98.7 jit_solution(13494405275530794970)
XLA Ops:
  0.0 0.7 pad_bitcast_fusion
  0.7 21.2 %all_to_all.15 = f32[128,1,128]{2,1,0:T(1,128)} all-to-all(f32[128,1,128]{2,1,0:T(1,128)S(1)} %broadcast_in_dim.9), channel_id=1, replica_groups=mesh['hemi'=2,'blk'=64] {'hemi','blk'}, dimensions={0} | all-to-all | bytes 131072 | tf_op jit(solution)/shard_map/all_to_all | solution.py:271
  21.9 3.5 %messenger.1 = f32[2,64,4,8,128]{4,3,2,1,0:T(8,128)} custom-call(f32[128,128]{1,0:T(8,128)} %bitcast.28, f32[2,128]{1,0:T(2,128)} %bitcast.35, f32[4,64,2,8,128]{4,3,2,1,0:T(8,128)} %bitcast.33, f32[4,64,2,8,128]{4,3,2,1,0:T(8,128)} %bitcast.34), custom_call_target="tpu_custom_call" | custom-call | flops 4194304 | bytes 6291456 | tf_op jit(solution)/shard_map/messenger/pallas_call | solution.py:93
  25.4 0.0 copy-start
  25.4 0.0 copy-start.1
  25.5 0.0 copy-start.2
  25.5 4.4 %all-to-all-start.1 = ((f32[128,32,128]{2,1,0:T(8,128)}), f32[128,32,128]{2,1,0:T(8,128)S(1)}, u32[]{:S(2)}, u32[]{:S(2)}) async-start(f32[128,32,128]{2,1,0:T(8,128)} %bitcast.32), calls=%async_computation.1 | async-start | bytes 4194304 | tf_op jit(solution)/shard_map/all_to_all | solution.py:274
  29.8 0.0 copy-done
  29.8 0.0 copy-done.1
  29.9 0.0 copy-done.2
  29.9 10.4 %gram.1.own_ref = f32[2,2,256,256]{3,2,1,0:T(8,128)S(1)} custom-call(s32[4]{0:T(128)S(1)} %copy-done.2, f32[128,128]{1,0:T(8,128)S(1)} %bitcast.29, f32[128,128]{1,0:T(8,128)S(1)} %bitcast.30, bf16[4,256,8192]{2,1,0:T(8,128)(2,1)} %bitcast.31), custom_call_target="tpu_custom_call" | custom-call | flops 4294967296 | bytes 17825792 | tf_op jit(solution)/shard_map/gram/pallas_call | solution.py:167
  40.2 1.1 %collective-permute-start = (f32[2,2,256,256]{3,2,1,0:T(8,128)S(1)}, f32[2,2,256,256]{3,2,1,0:T(8,128)S(1)}, u32[]{:S(2)}, u32[]{:S(2)}) collective-permute-start(f32[2,2,256,256]{3,2,1,0:T(8,128)S(1)} %gram.1.own_ref), channel_id=1, source_target_pairs={{0,64},{64,0},{1,65},{65,1},{2,66},{66,2},{3,67},{67,3},{4,68},{68... | collective-permute-start | bytes 3145736 | tf_op jit(solution)/shard_map/ppermute | solution.py:275
  41.4 2.3 %collective-permute-done.other_ref = f32[2,2,256,256]{3,2,1,0:T(8,128)S(1)} collective-permute-done((f32[2,2,256,256]{3,2,1,0:T(8,128)S(1)}, f32[2,2,256,256]{3,2,1,0:T(8,128)S(1)}, u32[]{:S(2)}, u32[]{:S(2)}) %collective-permute-start) | collective-permute-done | bytes 1048608 | tf_op jit(solution)/shard_map/ppermute | solution.py:275
  43.7 0.2 arrange.1.matrix_ref
  43.9 16.0 %all-to-all-done.1 = f32[128,32,128]{2,1,0:T(8,128)S(1)} async-done(((f32[128,32,128]{2,1,0:T(8,128)}), f32[128,32,128]{2,1,0:T(8,128)S(1)}, u32[]{:S(2)}, u32[]{:S(2)}) %all-to-all-start.1) | async-done | bytes 2097184 | tf_op jit(solution)/shard_map/all_to_all | solution.py:274
  59.9 1.3 %apply.1 = f32[4096,128]{1,0:T(8,128)S(1)} custom-call(bf16[2,2,2,256,256]{4,3,2,1,0:T(8,128)(2,1)S(1)} %arrange.1.matrix_ref, f32[4096,128]{1,0:T(8,128)S(1)} %bitcast.25), custom_call_target="tpu_custom_call" | custom-call | flops 536870912 | bytes 6291456 | tf_op jit(solution)/shard_map/apply/pallas_call | solution.py:234
  61.3 36.1 %all_to_all.16 = f32[128,32,128]{2,1,0:T(8,128)S(1)} all-to-all(f32[128,32,128]{2,1,0:T(8,128)S(1)} %bitcast.26), channel_id=1, replica_groups=mesh['hemi'=2,'blk'=64] {'hemi','blk'}, dimensions={0} | all-to-all | bytes 4194304 | tf_op jit(solution)/shard_map/all_to_all | solution.py:278
  97.3 1.4 %place.1 = f32[4,64,2,8,128]{4,3,2,1,0:T(8,128)} custom-call(f32[2,64,4,8,128]{4,3,2,1,0:T(8,128)S(1)} %bitcast.27), custom_call_target="tpu_custom_call" | custom-call | bytes 4194304 | tf_op jit(solution)/shard_map/place/pallas_call | solution.py:257
  (1 shorter events, 0.0 us)
Async XLA Ops:
  25.4 4.4 %copy-start = (f32[128,1,128]{2,1,0:T(1,128)S(1)}, f32[128,1,128]{2,1,0:T(1,128)}, u32[]{:S(2)}) copy-start(f32[128,1,128]{2,1,0:T(1,128)} %all_to_all.15) | copy-start | bytes 196612
  25.4 4.4 %copy-start.1 = (f32[16384]{0:T(1024)S(1)}, f32[16384]{0:T(1024)}, u32[]{:S(2)}) copy-start(f32[16384]{0:T(1024)} %param.11) | copy-start | bytes 196612
  25.5 4.4 %copy-start.2 = (s32[4]{0:T(128)S(1)}, s32[4]{0:T(128)}, u32[]{:S(2)}) copy-start(s32[4]{0:T(128)} %m_ref.1) | copy-start | bytes 52
  25.5 34.5 %all-to-all-start.1 = ((f32[128,32,128]{2,1,0:T(8,128)}), f32[128,32,128]{2,1,0:T(8,128)S(1)}, u32[]{:S(2)}, u32[]{:S(2)}) async-start(f32[128,32,128]{2,1,0:T(8,128)} %bitcast.32), calls=%async_computation.1 | async-start | bytes 4194304 | tf_op jit(solution)/shard_map/all_to_all | solution.py:274
  40.2 3.4 %collective-permute-start = (f32[2,2,256,256]{3,2,1,0:T(8,128)S(1)}, f32[2,2,256,256]{3,2,1,0:T(8,128)S(1)}, u32[]{:S(2)}, u32[]{:S(2)}) collective-permute-start(f32[2,2,256,256]{3,2,1,0:T(8,128)S(1)} %gram.1.own_ref), channel_id=1, source_target_pairs={{0,64},{64,0},{1,65},{65,1},{2,66},{66,2},{3,67},{67,3},{4,68},{68... | collective-permute-start | bytes 3145736 | tf_op jit(solution)/shard_map/ppermute | solution.py:275
